TPU v7x, 32 devices: a whole 2x2x4 slice. The times are simulated.
32 devices in a mesh: groups: 2 (over y), seq: 4 (over z), heads: 2 (over x), sub: 2 (over core).
Axes of the slice: x: 2, y: 2, z: 4, core: 2. Of those that a mesh axis runs over, the one named last changes fastest.
Arguments:
- queries: bfloat16 [8192, 1024], P(('groups', 'seq', 'heads'), 'sub'), parts along dimension 0, may hold values from -6 to 6
- keys: bfloat16 [8192, 1024], P(('groups', 'seq', 'heads'), 'sub'), parts along dimension 0, may hold values from -6 to 6
- values: bfloat16 [8192, 1024], P(('groups', 'seq', 'heads'), 'sub'), parts along dimension 0, may hold values from -6 to 6
- out_grad: bfloat16 [8192, 1024], P(('groups', 'seq', 'heads'), 'sub'), parts along dimension 0, may hold values from -6 to 6
- level_weights: float32 [8, 8, 8192], P('sub', None, ('groups', 'seq', 'heads')), parts along dimension 2, may hold values from 0.25 to 2
Outputs:
- grad_queries: bfloat16 [8192, 1024], P(('groups', 'seq', 'heads'), 'sub'), parts along dimension 0
- grad_keys: bfloat16 [8192, 1024], P(('groups', 'seq', 'heads'), 'sub'), parts along dimension 0
- grad_values: bfloat16 [8192, 1024], P(('groups', 'seq', 'heads'), 'sub'), parts along dimension 0
- weight_grads: float32 [8, 8, 8192], P('sub', None, ('groups', 'seq', 'heads')), parts along dimension 2
There are 2 independent parts, one for each index of `groups`. A program takes and returns all parts, laid end to end along the dimension named above; each array names one. Nothing has to cross between parts.
All inputs are finite; a program needn't handle non-finite values.
Results may differ from a plain program's by a relative error of at most 0.0056.
Values may be sent and summed in bfloat16 or wider, within the bound.
A program may use at most 64 MiB of HBM per device.

v0:
```python
import math

import jax
import jax.numpy as jnp
from jax import lax
from jax.sharding import PartitionSpec as P


def passed_along(block, axis, distance):
    devices = range(lax.axis_size(axis))
    route = [(i - distance, i) for i in devices if i - distance in devices]
    return lax.ppermute(block, axis, route)


def from_partner(shard, axis, apart):
    return lax.ppermute(shard, axis, [(i, i ^ 1 << apart) for i in range(lax.axis_size(axis))])


def top_state_move(block_sum, distance):
    return passed_along(block_sum.astype(jnp.bfloat16), ("seq", "heads"), distance)


def top_grad_move(pending, distance):
    return passed_along(pending, ("seq", "heads"), -distance)


def on_device(queries, keys, values, out_grad, level_weights):
    tok_rows = queries.shape[0]
    head_count = level_weights.shape[0]
    levels = level_weights.shape[1]
    head_width = queries.shape[1] // head_count
    shape_three = (tok_rows, head_count, head_width)
    queries_h = queries.reshape(shape_three)
    keys_h = keys.reshape(shape_three)
    values_h = values.reshape(shape_three)
    grads_h = out_grad.reshape(shape_three)
    bit_count = lax.axis_size(("seq", "heads")).bit_length() - 1
    position = lax.axis_index(("seq", "heads"))
    base_scale = 1.0 / math.sqrt(head_width * tok_rows)
    scales = [base_scale] + [
        base_scale / math.sqrt(2.0 ** (level_idx - 1)) for level_idx in range(1, levels)
    ]
    causal = jnp.tril(jnp.ones((tok_rows, tok_rows), dtype=bool))
    scores = jnp.einsum("thd,shd->hts", queries_h, keys_h, preferred_element_type=jnp.float32)
    grad_dots = jnp.einsum("thd,shd->hts", grads_h, values_h, preferred_element_type=jnp.float32)
    scores = jnp.where(causal, scores, 0.0)
    grad_dots = jnp.where(causal, grad_dots, 0.0)
    near_weight = scales[0] * jnp.sum(scores * grad_dots, axis=2)
    factor = scales[0] * level_weights[:, 0, :][:, :, None]
    grad_mix = (factor * grad_dots).astype(jnp.bfloat16)
    score_mix = (factor * scores).astype(jnp.bfloat16)
    grad_q = jnp.einsum("hts,shd->thd", grad_mix, keys_h, preferred_element_type=jnp.float32)
    near_k = jnp.einsum("hts,thd->shd", grad_mix, queries_h, preferred_element_type=jnp.float32)
    near_v = jnp.einsum("hts,thd->shd", score_mix, grads_h, preferred_element_type=jnp.float32)
    key_state = jnp.einsum("shd,she->hde", keys_h, values_h, preferred_element_type=jnp.float32)
    grad_list = []
    for level_idx in range(1, bit_count + 1):
        gate_now = level_weights[:, level_idx, :].T[:, :, None]
        scaled = (gate_now * queries_h).astype(jnp.bfloat16)
        grad_list.append(
            scales[level_idx]
            * jnp.einsum("thd,the->hde", scaled, grads_h, preferred_element_type=jnp.float32)
        )
    pending = jnp.stack(grad_list, axis=0)
    level_states = []
    reverse_sum = jnp.zeros_like(key_state)
    block_sum = key_state
    lower_bits = 0
    last_bit = bit_count - 1
    for bit_pos in range(lower_bits, last_bit):
        upper_half = position >> bit_pos & 1 == 1
        received = from_partner(block_sum, ("seq", "heads"), bit_pos)
        level_states.append(jnp.where(upper_half, received, 0.0))
        block_sum = block_sum + received
    for bit_pos in range(lower_bits, last_bit):
        upper_half = position >> bit_pos & 1 == 1
        received = from_partner(pending, ("seq", "heads"), bit_pos)
        reverse_sum = reverse_sum + jnp.where(upper_half, 0.0, received[0])
        pending = pending[1:] + received[1:]
    distance = lax.axis_size(("seq", "heads")) // 2
    top_state = top_state_move(block_sum, distance)
    level_states.append(top_state)
    top_grad = top_grad_move(pending, distance)
    reverse_sum = reverse_sum + top_grad[0]
    weight_rows = [near_weight]
    for level_idx in range(1, levels):
        if level_idx > bit_count:
            weight_rows.append(jnp.zeros_like(near_weight))
            continue
        state_low = level_states[level_idx - 1].astype(jnp.bfloat16)
        products = jnp.einsum(
            "the,hde->thd", grads_h, state_low, preferred_element_type=jnp.float32
        )
        gate_now = level_weights[:, level_idx, :].T[:, :, None]
        grad_q = grad_q + scales[level_idx] * gate_now * products
        weight_rows.append((scales[level_idx] * jnp.sum(products * queries_h, axis=2)).T)
    reverse_low = reverse_sum.astype(jnp.bfloat16)
    grad_k = near_k + jnp.einsum(
        "she,hde->shd", values_h, reverse_low, preferred_element_type=jnp.float32
    )
    grad_v = near_v + jnp.einsum(
        "shd,hde->she", keys_h, reverse_low, preferred_element_type=jnp.float32
    )
    flat = (tok_rows, head_count * head_width)
    weight_grads = jnp.stack(weight_rows, axis=1)
    return (
        grad_q.reshape(flat).astype(jnp.bfloat16),
        grad_k.reshape(flat).astype(jnp.bfloat16),
        grad_v.reshape(flat).astype(jnp.bfloat16),
        weight_grads,
    )


def solution(mesh):
    placed = (
        P(("groups", "seq", "heads"), "sub"),
        P(("groups", "seq", "heads"), "sub"),
        P(("groups", "seq", "heads"), "sub"),
        P(("groups", "seq", "heads"), "sub"),
        P("sub", None, ("groups", "seq", "heads")),
    )
    return jax.shard_map(
        on_device,
        mesh=mesh,
        in_specs=placed,
        out_specs=(
            P(("groups", "seq", "heads"), "sub"),
            P(("groups", "seq", "heads"), "sub"),
            P(("groups", "seq", "heads"), "sub"),
            P("sub", None, ("groups", "seq", "heads")),
        ),
        check_vma=False,
    )
```

profile of v0, /device:TPU:0, one launch (start us, length us, event | category | flops | bytes accessed | tf_op | source)
XLA Modules:
  0.0 67.8 jit_solution(12672516421317986934)
XLA Ops:
  0.6 0.0 copy-start
  0.6 1.0 %copy-done = bf16[512,512]{1,0:T(8,128)(2,1)S(1)} copy-done((bf16[512,512]{1,0:T(8,128)(2,1)S(1)}, bf16[512,512]{1,0:T(8,128)(2,1)}, u32[]{:S(2)}) %copy-start) | copy-done | bytes 524312
  1.7 2.1 %fusion.22 = f32[4,128,128]{2,1,0:T(8,128)} fusion(bf16[512,512]{1,0:T(8,128)(2,1)} %param.7, bf16[512,512]{1,0:T(8,128)(2,1)S(1)} %copy-done), kind=kOutput, calls=%fused_computation.41 | convolution fusion | flops 67108864 | bytes 1310720 | tf_op jit(solution)/shard_map/shd,she->hde/dot_general | solution.py:55
  3.8 3.0 %collective-permute-start = (f32[4,128,128]{2,1,0:T(8,128)}, f32[4,128,128]{2,1,0:T(8,128)}, u32[]{:S(2)}, u32[]{:S(2)}) collective-permute-start(f32[4,128,128]{2,1,0:T(8,128)} %fusion.22), channel_id=1, source_target_pairs={{0,2},{2,0},{4,6},{6,4},{8,10},{10,8},{12,14},{14,12},{1,3},{3,1},... | collective-permute-start | bytes 786440 | tf_op jit(solution)/shard_map/ppermute | solution.py:16
  6.7 1.3 %copy.73 = bf16[512,512]{0,1:T(8,128)(2,1)S(1)} copy(bf16[512,512]{1,0:T(8,128)(2,1)} %param.5) | data formatting | bytes 1048576 | tf_op args[0]
  8.0 1.3 %copy.101 = bf16[512,512]{0,1:T(8,128)(2,1)S(1)} copy(bf16[512,512]{1,0:T(8,128)(2,1)} %param.8) | data formatting | bytes 1048576 | tf_op jit(solution)/shard_map/reshape | solution.py:36
  9.3 1.0 %slice_multiply_fusion = (f32[4,1,512]{2,1,0:T(1,128)S(1)}, f32[4,1,512]{2,1,0:T(1,128)S(1)}, f32[4,1,512]{2,1,0:T(1,128)S(1)}, f32[4,1,512]{2,1,0:T(1,128)S(1)}) fusion(f32[4,8,512]{2,1,0:T(8,128)} %param.9), kind=kLoop, calls=%fused_computation.83 | loop fusion | flops 2048 | bytes 65536 | tf_op jit(solution)/shard_map/mul | solution.py:49
  10.3 0.3 fusion.9
  10.6 0.3 fusion.10
  10.9 0.3 fusion.11
  11.2 1.0 %pad_maximum_fusion = f32[3,4,128,128]{3,2,1,0:T(8,128)} fusion(f32[1,4,128,128]{3,2,1,0:T(8,128)S(1)} %fusion.9, f32[1,4,128,128]{3,2,1,0:T(8,128)S(1)} %fusion.10, f32[1,4,128,128]{3,2,1,0:T(8,128)S(1)} %fusion.11), kind=kLoop, calls=%fused_computation.39 | loop fusion | flops 393216 | bytes 1572864 | tf_op jit(solution)/shard_map/stack | solution.py:64
  12.2 0.1 collective-permute-start.3
  12.3 0.0 copy-done.4
  12.3 0.7 %fusion.24 = f32[4,512,512]{1,2,0:T(8,128)S(1)} fusion(bf16[512,4,128]{0,2,1:T(8,128)(2,1)S(1)} %bitcast.137, bf16[512,512]{1,0:T(8,128)(2,1)S(1)} %copy-done.4), kind=kOutput, calls=%fused_computation.43 | convolution fusion | flops 268435456 | bytes 5242880 | tf_op jit(solution)/shard_map/thd,shd->hts/dot_general | solution.py:45
  13.0 0.1 iota_compare_fusion
  13.1 0.9 %multiply_reduce_fusion = (f32[4,512]{1,0:T(4,128)S(1)}, f32[4,512,512]{1,2,0:T(8,128)S(1)}) fusion(f32[4,512,512]{1,2,0:T(8,128)S(1)} %fusion.24, pred[512,512]{0,1:T(8,128)(4,1)S(1)} %iota_compare_fusion, bf16[512,4,128]{0,2,1:T(8,128)(2,1)S(1)} %bitcast.145, bf16[512,512]{1,0:T(8,128)(2,1)S(1)} %copy-done), kind=kOutput, calls=%fused_computation | convolution fusion | flops 272627712 | bytes 9707520 | tf_op jit(solution)/shard_map/thd,shd->hts/dot_general | solution.py:44
  14.0 0.9 %copy-done.1 = f32[4,512,512]{1,2,0:T(8,128)} copy-done((f32[4,512,512]{1,2,0:T(8,128)}, f32[4,512,512]{1,2,0:T(8,128)S(1)}, u32[]{:S(2)}) %copy-start.1) | copy-done | bytes 4194328
  14.9 1.9 %convolution_bitcast_fusion.1 = f32[512,4,128]{0,2,1:T(8,128)} fusion(bf16[512,4,128]{0,2,1:T(8,128)(2,1)S(1)} %bitcast.146, f32[4,512,512]{1,2,0:T(8,128)S(1)} %fusion.24, f32[4,512]{1,0:T(4,128)S(1)} %bitcast.150, pred[512,512]{0,1:T(8,128)(4,1)S(1)} %iota_compare_fusion), kind=kOutput, calls=%fused_computation.14 | convolution fusion | flops 271581184 | bytes 6037504 | tf_op jit(solution)/shard_map/hts,thd->shd/dot_general | solution.py:53
  16.8 0.9 %fusion.4 = f32[512,4,128]{0,2,1:T(8,128)S(1)} fusion(bf16[512,4,128]{0,2,1:T(8,128)(2,1)S(1)} %bitcast.138, f32[4,512,512]{1,2,0:T(8,128)S(1)} %get-tuple-element.24, f32[4,512]{1,0:T(4,128)S(1)} %bitcast.151, pred[512,512]{0,1:T(8,128)(4,1)S(1)} %iota_compare_fusion), kind=kOutput, calls=%fused_computation.15 | convolution fusion | flops 271581184 | bytes 6037504 | tf_op jit(solution)/shard_map/hts,thd->shd/dot_general | solution.py:54
  17.8 0.0 collective-permute-done
  17.8 1.1 %add.40 = f32[4,128,128]{2,1,0:T(8,128)S(1)} add(f32[4,128,128]{2,1,0:T(8,128)} %fusion.22, f32[4,128,128]{2,1,0:T(8,128)} %collective-permute-done) | non-fusion elementwise | flops 65536 | bytes 786432 | tf_op jit(solution)/shard_map/add | solution.py:74
  18.8 2.1 %collective-permute-start.1 = (f32[4,128,128]{2,1,0:T(8,128)S(1)}, f32[4,128,128]{2,1,0:T(8,128)S(1)}, u32[]{:S(2)}, u32[]{:S(2)}) collective-permute-start(f32[4,128,128]{2,1,0:T(8,128)S(1)} %add.40), channel_id=1, source_target_pairs={{0,4},{2,6},{4,0},{6,2},{8,12},{10,14},{12,8},{14,10},{1,5},{3,7},... | collective-permute-start | bytes 786440 | tf_op jit(solution)/shard_map/ppermute | solution.py:16
  20.9 0.3 convolution_bitcast_fusion.6
  21.2 0.0 copy-start.2
  21.2 5.4 %collective-permute-done.1 = f32[4,128,128]{2,1,0:T(8,128)S(1)} collective-permute-done((f32[4,128,128]{2,1,0:T(8,128)S(1)}, f32[4,128,128]{2,1,0:T(8,128)S(1)}, u32[]{:S(2)}, u32[]{:S(2)}) %collective-permute-start.1) | collective-permute-done | bytes 262176 | tf_op jit(solution)/shard_map/ppermute | solution.py:16
  26.7 4.7 %collective-permute-start.2 = (bf16[4,128,128]{2,1,0:T(8,128)(2,1)S(1)}, bf16[4,128,128]{2,1,0:T(8,128)(2,1)S(1)}, u32[]{:S(2)}, u32[]{:S(2)}) collective-permute-start(bf16[4,128,128]{2,1,0:T(8,128)(2,1)S(1)} %add_convert_fusion.1), channel_id=1, source_target_pairs={{0,8},{2,10},{4,12},{6,14},{1,9},{3,11},{5,13},{7,15},{16,24},{18,... | collective-permute-start | bytes 393224 | tf_op jit(solution)/shard_map/ppermute | solution.py:12
  31.4 0.3 convolution_bitcast_fusion.5
  31.7 0.0 collective-permute-done.3
  31.7 1.1 %slice_add_fusion = f32[2,4,128,128]{3,2,1,0:T(8,128)S(1)} fusion(f32[3,4,128,128]{3,2,1,0:T(8,128)} %collective-permute-done.3, f32[1,4,128,128]{3,2,1,0:T(8,128)S(1)} %fusion.9, f32[1,4,128,128]{3,2,1,0:T(8,128)S(1)} %fusion.10), kind=kLoop, calls=%fused_computation.50 | loop fusion | flops 262144 | bytes 1572864 | tf_op jit(solution)/shard_map/add | solution.py:79
  32.8 1.6 %collective-permute-start.4 = (f32[2,4,128,128]{3,2,1,0:T(8,128)S(1)}, f32[2,4,128,128]{3,2,1,0:T(8,128)S(1)}, u32[]{:S(2)}, u32[]{:S(2)}) collective-permute-start(f32[2,4,128,128]{3,2,1,0:T(8,128)S(1)} %slice_add_fusion), channel_id=1, source_target_pairs={{0,4},{2,6},{4,0},{6,2},{8,12},{10,14},{12,8},{14,10},{1,5},{3,7},... | collective-permute-start | bytes 1572872 | tf_op jit(solution)/shard_map/ppermute | solution.py:16
  34.4 0.2 collective-permute-done.2
  34.7 0.4 fusion.17
  35.1 0.0 copy-done.2
  35.1 0.0 copy-start.3
  35.1 0.0 copy-start.5
  35.1 1.9 %add_convert_fusion = bf16[512,4,128]{0,2,1:T(8,128)(2,1)} fusion(f32[512,4,128]{0,2,1:T(8,128)S(1)} %get-tuple-element.25, f32[512,4,128]{0,2,1:T(8,128)S(1)} %convolution_bitcast_fusion.5, f32[512,4,128]{0,2,1:T(8,128)S(1)} %convolution_bitcast_fusion.6, f32[512,4]{0,1:T(4,128)S(1)} %get-tuple-element.30, f32[512,4]{0,1:T(4,128)S(1)} %get-tuple-element.31, ...), kind=kOutput, calls=%fused_computation.37 | convolution fusion | flops 273416192 | bytes 8683520 | tf_op jit(solution)/shard_map/hts,shd->thd/dot_general | solution.py:52
  37.0 8.2 %collective-permute-done.4 = f32[2,4,128,128]{3,2,1,0:T(8,128)S(1)} collective-permute-done((f32[2,4,128,128]{3,2,1,0:T(8,128)S(1)}, f32[2,4,128,128]{3,2,1,0:T(8,128)S(1)}, u32[]{:S(2)}, u32[]{:S(2)}) %collective-permute-start.4) | collective-permute-done | bytes 524320 | tf_op jit(solution)/shard_map/ppermute | solution.py:16
  45.2 0.8 %copy-done.6 = f32[2,4,128,128]{3,2,1,0:T(8,128)} copy-done((f32[2,4,128,128]{3,2,1,0:T(8,128)}, f32[2,4,128,128]{3,2,1,0:T(8,128)S(1)}, u32[]{:S(2)}) %copy-start.6) | copy-done | bytes 524312
  46.0 1.3 %collective-permute-start.5 = (f32[1,4,128,128]{3,2,1,0:T(8,128)S(1)}, f32[1,4,128,128]{3,2,1,0:T(8,128)}, u32[]{:S(2)}, u32[]{:S(2)}) collective-permute-start(f32[1,4,128,128]{3,2,1,0:T(8,128)S(1)} %slice_add_fusion.1), channel_id=1, source_target_pairs={{8,0},{10,2},{12,4},{14,6},{9,1},{11,3},{13,5},{15,7},{24,16},{26,... | collective-permute-start | bytes 786440 | tf_op jit(solution)/shard_map/ppermute | solution.py:12
  47.3 2.0 %copy.89 = bf16[512,512]{1,0:T(8,128)(2,1)} copy(bf16[512,512]{0,1:T(8,128)(2,1)} %bitcast.147) | data formatting | bytes 1048576
  49.4 0.7 %stack.39 = f32[4,8,512]{2,1,0:T(8,128)} concatenate(f32[4,1,512]{2,1,0:T(1,128)S(1)} %copy.85, f32[4,1,512]{2,1,0:T(1,128)S(1)} %copy.86, f32[4,1,512]{2,1,0:T(1,128)S(1)} %copy.87, f32[4,1,512]{2,1,0:T(1,128)S(1)} %copy.88, f32[4,4,512]{2,1,0:T(4,128)S(1)} %stack.38), dimensions={1} | concatenate | bytes 131072 | tf_op jit(solution)/shard_map/stack | solution.py:105
  50.1 12.0 %collective-permute-done.5 = f32[1,4,128,128]{3,2,1,0:T(8,128)} collective-permute-done((f32[1,4,128,128]{3,2,1,0:T(8,128)S(1)}, f32[1,4,128,128]{3,2,1,0:T(8,128)}, u32[]{:S(2)}, u32[]{:S(2)}) %collective-permute-start.5) | collective-permute-done | bytes 262176 | tf_op jit(solution)/shard_map/ppermute | solution.py:12
  62.1 1.2 %fusion.46 = bf16[4,128,128]{2,1,0:T(8,128)(2,1)S(1)} fusion(f32[1,4,128,128]{3,2,1,0:T(8,128)} %collective-permute-done.5, f32[2,4,128,128]{3,2,1,0:T(8,128)} %copy-done.6, f32[3,4,128,128]{3,2,1,0:T(8,128)} %collective-permute-done.3, pred[]{:T(512)S(6)} %eq.9, pred[]{:T(512)S(6)} %eq.8), kind=kLoop, calls=%fused_computation.70 | loop fusion | flops 327680 | bytes 917506 | tf_op jit(solution)/shard_map/convert_element_type | solution.py:97
  63.3 0.0 copy-done.3
  63.3 1.1 %fusion.7 = bf16[512,4,128]{0,2,1:T(8,128)(2,1)} fusion(f32[512,4,128]{0,2,1:T(8,128)S(1)} %copy-done.3, bf16[4,128,128]{2,1,0:T(8,128)(2,1)S(1)} %fusion.46, bf16[512,512]{1,0:T(8,128)(2,1)S(1)} %copy-done.5), kind=kOutput, calls=%fused_computation.23 | convolution fusion | flops 67633152 | bytes 2228224 | tf_op jit(solution)/shard_map/she,hde->shd/dot_general | solution.py:98
  64.4 2.0 %copy.90 = bf16[512,512]{1,0:T(8,128)(2,1)} copy(bf16[512,512]{0,1:T(8,128)(2,1)} %bitcast.149) | data formatting | bytes 1048576
  66.4 0.3 fusion.8
  66.8 1.0 %copy.91 = bf16[512,512]{1,0:T(8,128)(2,1)} copy(bf16[512,512]{0,1:T(8,128)(2,1)S(1)} %bitcast.148) | data formatting | bytes 1048576
  (19 shorter events, 0.2 us)
Async XLA Ops:
  0.6 1.0 %copy-start = (bf16[512,512]{1,0:T(8,128)(2,1)S(1)}, bf16[512,512]{1,0:T(8,128)(2,1)}, u32[]{:S(2)}) copy-start(bf16[512,512]{1,0:T(8,128)(2,1)} %param.6) | copy-start | bytes 1572868
  3.8 8.5 %copy-start.4 = (bf16[512,512]{1,0:T(8,128)(2,1)S(1)}, bf16[512,512]{1,0:T(8,128)(2,1)}, u32[]{:S(2)}) copy-start(bf16[512,512]{1,0:T(8,128)(2,1)} %param.7) | copy-start | bytes 1572868
  3.8 14.0 %collective-permute-start = (f32[4,128,128]{2,1,0:T(8,128)}, f32[4,128,128]{2,1,0:T(8,128)}, u32[]{:S(2)}, u32[]{:S(2)}) collective-permute-start(f32[4,128,128]{2,1,0:T(8,128)} %fusion.22), channel_id=1, source_target_pairs={{0,2},{2,0},{4,6},{6,4},{8,10},{10,8},{12,14},{14,12},{1,3},{3,1},... | collective-permute-start | bytes 786440 | tf_op jit(solution)/shard_map/ppermute | solution.py:16
  12.2 19.5 %collective-permute-start.3 = (f32[3,4,128,128]{3,2,1,0:T(8,128)}, f32[3,4,128,128]{3,2,1,0:T(8,128)}, u32[]{:S(2)}, u32[]{:S(2)}) collective-permute-start(f32[3,4,128,128]{3,2,1,0:T(8,128)} %pad_maximum_fusion), channel_id=1, source_target_pairs={{0,2},{2,0},{4,6},{6,4},{8,10},{10,8},{12,14},{14,12},{1,3},{3,1},... | collective-permute-start | bytes 2359304 | tf_op jit(solution)/shard_map/ppermute | solution.py:16
  12.9 1.9 %copy-start.1 = (f32[4,512,512]{1,2,0:T(8,128)}, f32[4,512,512]{1,2,0:T(8,128)S(1)}, u32[]{:S(2)}) copy-start(f32[4,512,512]{1,2,0:T(8,128)S(1)} %fusion.24) | copy-start | bytes 12582916
  18.8 7.8 %collective-permute-start.1 = (f32[4,128,128]{2,1,0:T(8,128)S(1)}, f32[4,128,128]{2,1,0:T(8,128)S(1)}, u32[]{:S(2)}, u32[]{:S(2)}) collective-permute-start(f32[4,128,128]{2,1,0:T(8,128)S(1)} %add.40), channel_id=1, source_target_pairs={{0,4},{2,6},{4,0},{6,2},{8,12},{10,14},{12,8},{14,10},{1,5},{3,7},... | collective-permute-start | bytes 786440 | tf_op jit(solution)/shard_map/ppermute | solution.py:16
  21.2 13.9 %copy-start.2 = (f32[4,512,512]{1,2,0:T(8,128)S(1)}, f32[4,512,512]{1,2,0:T(8,128)}, u32[]{:S(2)}) copy-start(f32[4,512,512]{1,2,0:T(8,128)} %copy-done.1) | copy-start | bytes 12582916
  26.7 7.9 %collective-permute-start.2 = (bf16[4,128,128]{2,1,0:T(8,128)(2,1)S(1)}, bf16[4,128,128]{2,1,0:T(8,128)(2,1)S(1)}, u32[]{:S(2)}, u32[]{:S(2)}) collective-permute-start(bf16[4,128,128]{2,1,0:T(8,128)(2,1)S(1)} %add_convert_fusion.1), channel_id=1, source_target_pairs={{0,8},{2,10},{4,12},{6,14},{1,9},{3,11},{5,13},{7,15},{16,24},{18,... | collective-permute-start | bytes 393224 | tf_op jit(solution)/shard_map/ppermute | solution.py:12
  32.8 12.4 %collective-permute-start.4 = (f32[2,4,128,128]{3,2,1,0:T(8,128)S(1)}, f32[2,4,128,128]{3,2,1,0:T(8,128)S(1)}, u32[]{:S(2)}, u32[]{:S(2)}) collective-permute-start(f32[2,4,128,128]{3,2,1,0:T(8,128)S(1)} %slice_add_fusion), channel_id=1, source_target_pairs={{0,4},{2,6},{4,0},{6,2},{8,12},{10,14},{12,8},{14,10},{1,5},{3,7},... | collective-permute-start | bytes 1572872 | tf_op jit(solution)/shard_map/ppermute | solution.py:16
  35.1 28.2 %copy-start.3 = (f32[512,4,128]{0,2,1:T(8,128)S(1)}, f32[512,4,128]{0,2,1:T(8,128)}, u32[]{:S(2)}) copy-start(f32[512,4,128]{0,2,1:T(8,128)} %convolution_bitcast_fusion.1) | copy-start | bytes 3145732
  35.1 28.2 %copy-start.5 = (bf16[512,512]{1,0:T(8,128)(2,1)S(1)}, bf16[512,512]{1,0:T(8,128)(2,1)}, u32[]{:S(2)}) copy-start(bf16[512,512]{1,0:T(8,128)(2,1)} %param.7) | copy-start | bytes 1572868
  45.2 0.8 %copy-start.6 = (f32[2,4,128,128]{3,2,1,0:T(8,128)}, f32[2,4,128,128]{3,2,1,0:T(8,128)S(1)}, u32[]{:S(2)}) copy-start(f32[2,4,128,128]{3,2,1,0:T(8,128)S(1)} %collective-permute-done.4) | copy-start | bytes 1572868
  46.0 16.1 %collective-permute-start.5 = (f32[1,4,128,128]{3,2,1,0:T(8,128)S(1)}, f32[1,4,128,128]{3,2,1,0:T(8,128)}, u32[]{:S(2)}, u32[]{:S(2)}) collective-permute-start(f32[1,4,128,128]{3,2,1,0:T(8,128)S(1)} %slice_add_fusion.1), channel_id=1, source_target_pairs={{8,0},{10,2},{12,4},{14,6},{9,1},{11,3},{13,5},{15,7},{24,16},{26,... | collective-permute-start | bytes 786440 | tf_op jit(solution)/shard_map/ppermute | solution.py:12
where the time goes:
time: 68.4 us; the launch traced here: 67.8 us
  waiting for transfers between devices  25.9 us (38%)
  starting transfers between devices  12.7 us (19%)
  matrix products  11.7 us (17%)
  local copies, waits for them, and re-layouts  11.1 us (16%)
  other arithmetic  5.45 us (8%)
  between operations  0.92 us (1%)
    ppermute x4, waiting for transfers between devices, from_partner(): lax.ppermute(shard, axis, [(i, i ^ 1 << apart) for i in range(lax.axis_si...  13.7 us
    ppermute x2, waiting for transfers between devices, passed_along(): return lax.ppermute(block, axis, route)  12.2 us
    unnamed x20, local copies, waits for them, and re-layouts  9.08 us
    ppermute x4, starting transfers between devices, from_partner(): lax.ppermute(shard, axis, [(i, i ^ 1 << apart) for i in range(lax.axis_si...  6.78 us
    ppermute x2, starting transfers between devices, passed_along(): return lax.ppermute(block, axis, route)  5.95 us
    dot_general x1, matrix products, on_device(): jnp.einsum('shd,she->hde', keys_h, values_h, preferred_element_type=jnp.f...  2.09 us
    dot_general x1, matrix products, on_device(): jnp.einsum('hts,thd->shd', grad_mix, queries_h, preferred_element_type=jn...  1.89 us
    dot_general x1, matrix products, on_device(): jnp.einsum('hts,shd->thd', grad_mix, keys_h, preferred_element_type=jnp.f...  1.86 us
  transfers between devices with their start and end apart: 6, of which 4 were waited for; matrix products, arithmetic and copies ran while one was open for 26% of the time, Pallas kernels for 0%

commit v1 on v0

v1 whole, which is shorter than its diff:
```python
import functools
import math

import jax
import jax.numpy as jnp
from jax import lax
from jax.experimental import pallas as pl
from jax.experimental.pallas import tpu as pltpu
from jax.sharding import PartitionSpec as P

F32 = jnp.float32
BF16 = jnp.bfloat16
NN = (((1,), (0,)), ((), ()))
NT = (((1,), (1,)), ((), ()))


def mm(a, b, dims=NN):
    return lax.dot_general(a, b, dims, preferred_element_type=F32)


def kernel(
    dims,
    scales,
    q_hbm,
    k_hbm,
    v_hbm,
    g_hbm,
    lw_ref,
    gq_ref,
    gk_ref,
    gv_ref,
    wg_ref,
    q_s,
    k_s,
    v_s,
    g_s,
    qt_s,
    kt_s,
    nq_s,
    nk_s,
    nv_s,
    usum_s,
    tsum_s,
    p_s,
    u_send,
    u_recv,
    t_send,
    t_recv,
    in_sem,
    us_sem,
    ur_sem,
    ts_sem,
    tr_sem,
):
    bits, fine, heads, toks, width, levels = dims
    top = bits - 1
    pos = lax.axis_index("seq") * fine + lax.axis_index("heads")
    bit_of = [(pos // (1 << b)) % 2 for b in range(bits)]
    partner = [pos + (1 - 2 * bit_of[b]) * (1 << b) for b in range(bits)]
    is_upper = [bit_of[b] == 1 for b in range(bits)]

    def where_is(b):
        return {"seq": partner[b] // fine, "heads": partner[b] % fine}

    barrier = pltpu.get_barrier_semaphore()
    for b in range(bits):
        pl.semaphore_signal(
            barrier, inc=1, device_id=where_is(b), device_id_type=pl.DeviceIdType.MESH
        )

    pairs = [(k_hbm, k_s), (v_hbm, v_s), (q_hbm, q_s), (g_hbm, g_s)]
    loads = {}
    for half in (pairs[:2], pairs[2:]):
        for h in range(heads):
            for src, dst in half:
                i = 0 if dst is k_s else 1 if dst is v_s else 2 if dst is q_s else 3
                loads[i, h] = pltpu.make_async_copy(
                    src.at[:, pl.ds(h * width, width)], dst.at[h], in_sem.at[i, h]
                )
                loads[i, h].start()

    def u_copy(b, h):
        return pltpu.make_async_remote_copy(
            src_ref=u_send.at[b, h],
            dst_ref=u_recv.at[b, h],
            send_sem=us_sem.at[b, h],
            recv_sem=ur_sem.at[b, h],
            device_id=where_is(b),
            device_id_type=pl.DeviceIdType.MESH,
        )

    def t_copy(b, h):
        return pltpu.make_async_remote_copy(
            src_ref=t_send.at[b, h],
            dst_ref=t_recv.at[b, h],
            send_sem=ts_sem.at[b, h],
            recv_sem=tr_sem.at[b, h],
            device_id=where_is(b),
            device_id_type=pl.DeviceIdType.MESH,
        )

    def u_start(b, h):
        if b < top:
            u_copy(b, h).start()
        else:
            pl.when(jnp.logical_not(is_upper[b]))(lambda: u_copy(b, h).start())

    def u_wait(b, h):
        if b < top:
            u_copy(b, h).wait()
        else:
            pl.when(jnp.logical_not(is_upper[b]))(lambda: u_copy(b, h).wait_send())
            pl.when(is_upper[b])(lambda: u_copy(b, h).wait_recv())

    def t_start(b, h):
        if b < top:
            t_copy(b, h).start()
        else:
            pl.when(is_upper[b])(lambda: t_copy(b, h).start())

    def t_wait(b, h):
        if b < top:
            t_copy(b, h).wait()
        else:
            pl.when(is_upper[b])(lambda: t_copy(b, h).wait_send())
            pl.when(jnp.logical_not(is_upper[b]))(lambda: t_copy(b, h).wait_recv())

    blank = jnp.zeros((heads, width, width), BF16)

    @pl.when(is_upper[top])
    def _():
        t_recv[top] = blank

    @pl.when(jnp.logical_not(is_upper[top]))
    def _():
        u_recv[top] = blank

    def block_state(h):
        loads[0, h].wait()
        loads[1, h].wait()
        kt = k_s[h].T
        kt_s[h] = kt
        state = mm(kt, v_s[h])
        usum_s[h] = state
        u_send[0, h] = state.astype(BF16)

    def grad_states(h):
        loads[2, h].wait()
        loads[3, h].wait()
        qt = q_s[h].T
        qt_s[h] = qt
        qt32 = qt.astype(F32)
        for level in range(bits, 0, -1):
            scaled = (lw_ref[h, level : level + 1, :] * qt32).astype(BF16)
            state = scales[level] * mm(scaled, g_s[h])
            if level == bits:
                t_send[top, h] = state.astype(BF16)
                t_start(top, h)
            else:
                p_s[level - 1, h] = state

    tile = toks // 2
    row_idx = lax.broadcasted_iota(jnp.int32, (tile, tile), 0)
    col_idx = lax.broadcasted_iota(jnp.int32, (tile, tile), 1)
    causal = row_idx <= col_idx

    def near(h):
        a, c = slice(0, tile), slice(tile, toks)
        q, k, v, g, kt = q_s[h], k_s[h], v_s[h], g_s[h], kt_s[h]
        factor = scales[0] * lw_ref[h, 0:1, :]

        def piece(rows, cols, masked):
            w = mm(k[rows], q[cols], NT)
            y = mm(v[rows], g[cols], NT)
            if masked:
                w = jnp.where(causal, w, 0.0)
                y = jnp.where(causal, y, 0.0)
            near_w = jnp.sum(w * y, axis=0, keepdims=True)
            f = factor[:, cols]
            return (f * y).astype(BF16), (f * w).astype(BF16), near_w

        gm_aa, sm_aa, nw_aa = piece(a, a, True)
        gm_ac, sm_ac, nw_ac = piece(a, c, False)
        gm_cc, sm_cc, nw_cc = piece(c, c, True)
        wg_ref[h, 0:1, a] = scales[0] * nw_aa
        wg_ref[h, 0:1, c] = scales[0] * (nw_ac + nw_cc)
        nq_s[h, :, a] = mm(kt[:, a], gm_aa)
        nq_s[h, :, c] = mm(kt[:, a], gm_ac) + mm(kt[:, c], gm_cc)
        nk_s[h, a, :] = mm(gm_aa, q[a]) + mm(gm_ac, q[c])
        nk_s[h, c, :] = mm(gm_cc, q[c])
        nv_s[h, a, :] = mm(sm_aa, g[a]) + mm(sm_ac, g[c])
        nv_s[h, c, :] = mm(sm_cc, g[c])

    def far_level(level, h):
        state = u_recv[level - 1, h]
        if level - 1 < top:
            state = jnp.where(is_upper[level - 1], state, jnp.zeros_like(state))
        products = mm(state, g_s[h], NT)
        row = jnp.sum(products * qt_s[h].astype(F32), axis=0, keepdims=True)
        wg_ref[h, level : level + 1, :] = scales[level] * row
        return (scales[level] * lw_ref[h, level : level + 1, :]) * products

    def u_round(r, h):
        u_wait(r, h)
        if r < top:
            total = usum_s[h] + u_recv[r, h].astype(F32)
            usum_s[h] = total
            u_send[r + 1, h] = total.astype(BF16)
            u_start(r + 1, h)

    def t_round(r, h):
        b = top - r
        t_wait(b, h)
        total = t_recv[b, h].astype(F32)
        if r > 0:
            total = tsum_s[h] + total
        if b > 0:
            tsum_s[h] = total
            extra = p_s[b - 1, h]
            total = total + jnp.where(is_upper[b - 1], extra, jnp.zeros_like(extra))
            t_send[b - 1, h] = total.astype(BF16)
            t_start(b - 1, h)
        return total

    for h in range(heads):
        block_state(h)
        if h == 0:
            pl.semaphore_wait(barrier, bits)
        u_start(0, h)
    for h in range(heads):
        grad_states(h)
    if bits + 1 < levels:
        wg_ref[:, bits + 1 :, :] = jnp.zeros((heads, levels - bits - 1, toks), F32)
    pending = [(level, h) for level in range(1, bits) for h in range(heads)]
    for r in range(bits):
        for h in range(heads):
            if h * bits // heads == r:
                near(h)
        for level, h in list(pending):
            if level <= r and h * bits // heads <= r:
                nq_s[h] += far_level(level, h)
                pending.remove((level, h))
        if r < top:
            for h in range(heads):
                u_round(r, h)
                t_round(r, h)
    for h in range(heads):
        cols = slice(h * width, (h + 1) * width)
        u_round(top, h)
        gq_ref[:, cols] = (nq_s[h] + far_level(bits, h)).astype(BF16).T
        low = t_round(top, h).astype(BF16)
        gk_ref[:, cols] = (nk_s[h] + mm(v_s[h], low, NT)).astype(BF16)
        gv_ref[:, cols] = (nv_s[h] + mm(k_s[h], low)).astype(BF16)


def on_device(queries, keys, values, out_grad, level_weights):
    toks, flat = queries.shape
    heads, levels = level_weights.shape[:2]
    width = flat // heads
    fine = lax.axis_size("heads")
    bits = (lax.axis_size("seq") * fine).bit_length() - 1
    base = 1.0 / math.sqrt(width * toks)
    scales = [base] + [base / math.sqrt(2.0 ** (i - 1)) for i in range(1, levels)]
    dims = (bits, fine, heads, toks, width, levels)
    hbm = pl.BlockSpec(memory_space=pltpu.MemorySpace.HBM)
    vmem = pl.BlockSpec(memory_space=pltpu.MemorySpace.VMEM)
    tok_major = pltpu.VMEM((heads, toks, width), BF16)
    feat_major = pltpu.VMEM((heads, width, toks), BF16)
    state = pltpu.VMEM((heads, width, width), F32)
    slots = pltpu.VMEM((bits, heads, width, width), BF16)
    sems = pltpu.SemaphoreType.DMA((bits, heads))
    return pl.pallas_call(
        functools.partial(kernel, dims, scales),
        out_shape=(
            jax.ShapeDtypeStruct((toks, flat), BF16),
            jax.ShapeDtypeStruct((toks, flat), BF16),
            jax.ShapeDtypeStruct((toks, flat), BF16),
            jax.ShapeDtypeStruct((heads, levels, toks), F32),
        ),
        in_specs=[hbm, hbm, hbm, hbm, vmem],
        out_specs=(vmem, vmem, vmem, vmem),
        scratch_shapes=[
            tok_major,
            tok_major,
            tok_major,
            tok_major,
            feat_major,
            feat_major,
            pltpu.VMEM((heads, width, toks), F32),
            pltpu.VMEM((heads, toks, width), F32),
            pltpu.VMEM((heads, toks, width), F32),
            state,
            state,
            pltpu.VMEM((max(bits - 1, 1), heads, width, width), F32),
            slots,
            slots,
            slots,
            slots,
            pltpu.SemaphoreType.DMA((4, heads)),
            sems,
            sems,
            sems,
            sems,
        ],
        compiler_params=pltpu.CompilerParams(
            collective_id=0, has_side_effects=True, vmem_limit_bytes=40 * 1024 * 1024
        ),
    )(queries, keys, values, out_grad, level_weights)


def solution(mesh):
    rows = P(("groups", "seq", "heads"), "sub")
    weights = P("sub", None, ("groups", "seq", "heads"))
    return jax.shard_map(
        on_device,
        mesh=mesh,
        in_specs=(rows, rows, rows, rows, weights),
        out_specs=(rows, rows, rows, weights),
        check_vma=False,
    )
```

time: 68.4 us -> 30.9 us (0.45)
  waiting for transfers between devices: 25.9 us -> 0 us
  Pallas kernels: 0 us -> 21.9 us
  starting transfers between devices: 12.7 us -> 0 us
  matrix products: 11.7 us -> 0 us
  other arithmetic: 5.45 us -> 0 us
  local copies, waits for them, and re-layouts: 11.1 us -> 8.01 us
    ppermute x6 -> x0, waiting for transfers between devices: 25.9 us -> none  [the longest x4 13.7 us: from_partner(): lax.ppermute(shard, axis, [(i, i ^ 1 << apart) for i in range(lax.axis_si...]
    pallas_call x0 -> x1, Pallas kernels: none -> 21.9 us  [on_device(): pl.pallas_call(functools.partial(kernel, dims, scales), out_shape=(jax.Sh...]
    ppermute x6 -> x0, starting transfers between devices: 12.7 us -> none  [the longest x4 6.78 us: from_partner(): lax.ppermute(shard, axis, [(i, i ^ 1 << apart) for i in range(lax.axis_si...]
    dot_general x14 -> x0, matrix products: 11.7 us -> none  [the longest x1 2.09 us: on_device(): jnp.einsum('shd,she->hde', keys_h, values_h, preferred_element_type=jnp.f...]
    add x3 -> x0, other arithmetic: 2.19 us -> none  [the longest x2 1.13 us: on_device(): pending = pending[1:] + received[1:]]
    reshape x1 -> x0, local copies, waits for them, and re-layouts: 1.26 us -> none  [on_device(): grads_h = out_grad.reshape(shape_three)]
    convert_element_type x2 -> x0, other arithmetic: 1.19 us -> none  [the longest x1 1.16 us: on_device(): reverse_low = reverse_sum.astype(jnp.bfloat16)]
    unnamed x20 -> x14, local copies, waits for them, and re-layouts: 9.08 us -> 8.01 us
  transfers between devices with their start and end apart: 6 -> 0, of which waited for: 4 -> 0; matrix products, arithmetic and copies ran while one was open for 26% -> 0% of each run, Pallas kernels for 0% -> 0%
where the time goes in v1:
time: 30.9 us; the launch traced here: 30.6 us
  Pallas kernels  21.9 us (71%)
  local copies, waits for them, and re-layouts  8.01 us (26%)
  between operations  0.65 us (2%)
    pallas_call x1, Pallas kernels, on_device(): pl.pallas_call(functools.partial(kernel, dims, scales), out_shape=(jax.Sh...  21.9 us
    unnamed x14, local copies, waits for them, and re-layouts  8.01 us

profile of v1, /device:TPU:0, one launch (start us, length us, event | category | flops | bytes accessed | tf_op | source)
XLA Modules:
  0.0 30.6 jit_solution(9821103075425761116)
XLA Ops:
  0.6 0.0 copy-start
  0.6 1.0 %copy-done = bf16[512,512]{1,0:T(8,128)(2,1)S(1)} copy-done((bf16[512,512]{1,0:T(8,128)(2,1)S(1)}, bf16[512,512]{1,0:T(8,128)(2,1)}, u32[]{:S(2)}) %copy-start) | copy-done | bytes 524312
  1.7 0.0 copy-start.1
  1.7 1.0 %copy-done.1 = bf16[512,512]{1,0:T(8,128)(2,1)S(1)} copy-done((bf16[512,512]{1,0:T(8,128)(2,1)S(1)}, bf16[512,512]{1,0:T(8,128)(2,1)}, u32[]{:S(2)}) %copy-start.1) | copy-done | bytes 524312
  2.7 0.0 copy-start.2
  2.7 1.0 %copy-done.2 = bf16[512,512]{1,0:T(8,128)(2,1)S(1)} copy-done((bf16[512,512]{1,0:T(8,128)(2,1)S(1)}, bf16[512,512]{1,0:T(8,128)(2,1)}, u32[]{:S(2)}) %copy-start.2) | copy-done | bytes 524312
  3.8 0.0 copy-start.3
  3.8 1.0 %copy-done.3 = bf16[512,512]{1,0:T(8,128)(2,1)S(1)} copy-done((bf16[512,512]{1,0:T(8,128)(2,1)S(1)}, bf16[512,512]{1,0:T(8,128)(2,1)}, u32[]{:S(2)}) %copy-start.3) | copy-done | bytes 524312
  4.8 0.0 copy-start.4
  4.8 0.8 %copy-done.4 = f32[4,8,512]{2,1,0:T(8,128)S(1)} copy-done((f32[4,8,512]{2,1,0:T(8,128)S(1)}, f32[4,8,512]{2,1,0:T(8,128)}, u32[]{:S(2)}) %copy-start.4) | copy-done | bytes 65560
  5.6 21.9 %shard_map.84 = (bf16[512,512]{1,0:T(8,128)(2,1)S(1)}, bf16[512,512]{1,0:T(8,128)(2,1)S(1)}, bf16[512,512]{1,0:T(8,128)(2,1)S(1)}, f32[4,8,512]{2,1,0:T(8,128)S(1)}) custom-call(bf16[512,512]{1,0:T(8,128)(2,1)S(1)} %copy-done, bf16[512,512]{1,0:T(8,128)(2,1)S(1)} %copy-done.1, bf16[512,512]{1,0:T(8,128)(2,1)S(1)} %copy-done.2, ...), custom_call_target="tpu_custom_call" | custom-call | tf_op jit(solution)/shard_map/pallas_call | solution.py:272
  27.6 0.8 %copy.13 = bf16[512,512]{1,0:T(8,128)(2,1)} copy(bf16[512,512]{1,0:T(8,128)(2,1)S(1)} %get-tuple-element.8) | data formatting | bytes 1048576
  28.4 0.8 %copy.14 = bf16[512,512]{1,0:T(8,128)(2,1)} copy(bf16[512,512]{1,0:T(8,128)(2,1)S(1)} %get-tuple-element.9) | data formatting | bytes 1048576
  29.2 0.8 %copy.15 = bf16[512,512]{1,0:T(8,128)(2,1)} copy(bf16[512,512]{1,0:T(8,128)(2,1)S(1)} %get-tuple-element.10) | data formatting | bytes 1048576
  29.9 0.6 %copy.16 = f32[4,8,512]{2,1,0:T(8,128)} copy(f32[4,8,512]{2,1,0:T(8,128)S(1)} %get-tuple-element.11) | data formatting | bytes 131072
Async XLA Ops:
  0.6 1.0 %copy-start = (bf16[512,512]{1,0:T(8,128)(2,1)S(1)}, bf16[512,512]{1,0:T(8,128)(2,1)}, u32[]{:S(2)}) copy-start(bf16[512,512]{1,0:T(8,128)(2,1)} %q_hbm.1) | copy-start | bytes 1572868
  1.7 1.0 %copy-start.1 = (bf16[512,512]{1,0:T(8,128)(2,1)S(1)}, bf16[512,512]{1,0:T(8,128)(2,1)}, u32[]{:S(2)}) copy-start(bf16[512,512]{1,0:T(8,128)(2,1)} %k_hbm.1) | copy-start | bytes 1572868
  2.7 1.0 %copy-start.2 = (bf16[512,512]{1,0:T(8,128)(2,1)S(1)}, bf16[512,512]{1,0:T(8,128)(2,1)}, u32[]{:S(2)}) copy-start(bf16[512,512]{1,0:T(8,128)(2,1)} %v_hbm.1) | copy-start | bytes 1572868
  3.8 1.0 %copy-start.3 = (bf16[512,512]{1,0:T(8,128)(2,1)S(1)}, bf16[512,512]{1,0:T(8,128)(2,1)}, u32[]{:S(2)}) copy-start(bf16[512,512]{1,0:T(8,128)(2,1)} %g_hbm.1) | copy-start | bytes 1572868
  4.8 0.8 %copy-start.4 = (f32[4,8,512]{2,1,0:T(8,128)S(1)}, f32[4,8,512]{2,1,0:T(8,128)}, u32[]{:S(2)}) copy-start(f32[4,8,512]{2,1,0:T(8,128)} %lw_ref.1) | copy-start | bytes 196612
